TPU v7x, 512 devices: a whole 4x4x16 slice. The times are simulated.
512 devices in a mesh: ex: 128 (over y, x, z_lo), tok: 4 (over z_hi, core).
Axes of the slice: x: 4, y: 4, z: 16 (z_hi: 2, z_lo: 8; z = z_hi * 8 + z_lo), core: 2. Of those that a mesh axis runs over, the one named last changes fastest.
Arguments:
- proj_rows: bfloat16 [1048576, 128], P(('ex', 'tok')), may hold values from -6 to 6
- query_features: bfloat16 [8192, 4096], P('ex'), may hold values from -0.09375 to 0.09375
- doc_lengths: int32 [128, 32], P('ex'), may hold values from 1 to 4096, 8192 in all within a row
- owner_map: int32 [128, 32], P('ex'), may hold values from 0 to 31, each once within a row
Outputs:
- scores: float32 [8192, 4096], P('ex', 'tok')
Inputs may be any that keep to these rules, and one draw needn't show every extreme that they name: `owner_map`: each row lists the slots 0 to 31 once each. `doc_lengths`: each row sums to 8192; its largest entry is exactly 4096.
All inputs are finite; a program needn't handle non-finite values.
Results may differ from a plain program's by a relative error of at most 0.0029.
Values may be sent and summed in bfloat16 or wider, within the bound.
A program may use at most 64 MiB of HBM per device.

v0:
```python
import jax
import jax.numpy as jnp
from jax import lax
from jax.sharding import PartitionSpec as P


def slot_lookup(lengths, owner_slots, positions):
    doc_ends = jnp.cumsum(lengths)
    doc_index = jnp.sum((positions[:, None] >= doc_ends[None, :]).astype(jnp.int32), axis=1)
    doc_match = doc_index[:, None] == jnp.arange(lengths.shape[0], dtype=jnp.int32)[None, :]
    return jnp.sum(jnp.where(doc_match, owner_slots[None, :], 0), axis=1)


def kron_sums(row_data, slots, targets):
    proj_width = row_data.shape[1] // 2
    count = row_data.shape[0]
    input_rows = row_data[:, :proj_width]
    grad_rows = row_data[:, proj_width:]

    def slot_group(slot_set):
        slot_mask = (slots[:, None] == slot_set[None, :]).astype(jnp.bfloat16)
        spread = (slot_mask[:, :, None] * grad_rows[:, None, :]).reshape(count, 4 * proj_width)
        return jnp.einsum("ta,tb->ab", spread, input_rows, preferred_element_type=jnp.float32)

    result = lax.map(slot_group, targets.reshape(-1, 4))
    return result.reshape(targets.shape[0], proj_width * proj_width)


def body(proj_rows, query_features, doc_lengths, owner_map):
    lengths = doc_lengths[0]
    owner_slots = owner_map[0]
    tok_count = lax.axis_size("tok")
    doc_dev = owner_slots.shape[0] // tok_count
    tok_index = lax.axis_index("tok")
    targets = tok_index * doc_dev + jnp.arange(doc_dev, dtype=jnp.int32)
    portion = lax.all_gather(proj_rows, "tok", axis=0, tiled=True)
    positions = jnp.arange(portion.shape[0], dtype=jnp.int32)
    summed = kron_sums(portion, slot_lookup(lengths, owner_slots, positions), targets)
    own_lengths = jnp.sum(
        jnp.where(owner_slots[None, :] == targets[:, None], lengths[None, :], 0), axis=1
    )
    features = (summed / jnp.sqrt(own_lengths.astype(jnp.float32))[:, None]).astype(jnp.bfloat16)
    return jnp.einsum(
        "qf,df->qd",
        query_features,
        lax.all_gather(features, "ex", axis=0, tiled=True),
        preferred_element_type=jnp.float32,
    )


def solution(mesh):
    placed = (P(("ex", "tok"), None), P("ex", None), P("ex", None), P("ex", None))
    return jax.shard_map(
        body, mesh=mesh, in_specs=placed, out_specs=P("ex", "tok"), check_vma=False
    )
```

profile of v0, /device:TPU:0, one launch (start us, length us, event | category | flops | bytes accessed | tf_op | source)
XLA Modules:
  0.0 1094.7 jit_solution(13539632485198462072)
XLA Ops:
  6.5 0.0 copy-start
  6.5 0.0 all-gather.3.cloned.1.call-start
  6.5 0.7 all-gather.3.cloned.1.call-update
  7.3 0.0 all-gather.5.cloned.1.call-start
  7.3 0.7 copy.9
  8.1 0.1 reduce-window.8
  8.1 0.1 reduce
  8.3 0.9 select_reduce_fusion.1
  9.1 0.2 convert_reduce_fusion
  9.3 0.9 select_reduce_fusion
  10.3 74.3 %all-gather.3.cloned.1.call-done = bf16[8192,128]{1,0:T(8,128)(2,1)} async-done(((bf16[2048,128]{1,0:T(8,128)(2,1)}), bf16[8192,128]{1,0:T(8,128)(2,1)}) %all-gather.3.cloned.1.call-update) | async-done | bytes 2097168 | tf_op jit(solution)/shard_map/all_gather | solution.py:36
  84.5 4.3 fusion.2
  88.8 2.7 copy.10
  91.5 6.2 while.10
  91.5 0.1 compare_convert_fusion.2
  91.6 1.6 broadcast_multiply_fusion.2
  93.2 1.4 fusion.14
  94.6 0.1 compare_convert_fusion.2
  94.7 1.6 broadcast_multiply_fusion.2
  96.3 1.4 fusion.14
  97.7 0.1 copy.11
  97.9 0.1 reshape.75
  98.0 0.7 divide_convert_fusion
  98.7 0.0 all-gather.5.cloned.1.call-update
  98.7 982.3 %all-gather.5.cloned.1.call-done = bf16[1024,4096]{1,0:T(8,128)(2,1)} async-done(((bf16[8,4096]{1,0:T(8,128)(2,1)}), bf16[1024,4096]{1,0:T(8,128)(2,1)}) %all-gather.5.cloned.1.call-update) | async-done | bytes 8388624 | tf_op jit(solution)/shard_map/all_gather | solution.py:46
  1081.1 0.0 copy-done
  1081.1 6.7 convolution_bitcast_fusion.1
  (6 shorter events, 0.0 us)
Async XLA Ops:
  6.5 1074.5 %copy-start = (bf16[64,4096]{1,0:T(8,128)(2,1)S(1)}, bf16[64,4096]{1,0:T(8,128)(2,1)}, u32[]{:S(2)}) copy-start(bf16[64,4096]{1,0:T(8,128)(2,1)} %param.7) | copy-start | bytes 1572868
  6.5 78.0 %all-gather.3.cloned.1.call-start = ((), (), s32[]{:S(2)}) async-start(), calls=%async_computation | async-start | bytes 2621440 | tf_op jit(solution)/shard_map/all_gather | solution.py:36
  7.3 1073.8 %all-gather.5.cloned.1.call-start = ((), (), s32[]{:S(2)}) async-start(), calls=%async_computation.1 | async-start | bytes 8454144 | tf_op jit(solution)/shard_map/all_gather | solution.py:46
Sparse Core Ops, SparseCore 0:
  9.5 75.0 all-gather.2
  98.9 982.1 all-gather.4
where the time goes:
time: 1090 us
  waiting for transfers between devices  1060 us (97%)
  between operations  13.5 us (1%)
    all_gather x1, waiting for transfers between devices, body(): lax.all_gather(features, 'ex', axis=0, tiled=True)  982 us
    all_gather x1, waiting for transfers between devices, body(): portion = lax.all_gather(proj_rows, 'tok', axis=0, tiled=True)  74.3 us
  transfers between devices with their start and end apart: 2, of which 2 were waited for; matrix products, arithmetic and copies ran while one was open for 0% of the time, Pallas kernels for 0%

commit v1 on v0

--- a/solution.py
+++ b/solution.py
@@ -43,7 +43,9 @@
     return jnp.einsum(
         "qf,df->qd",
         query_features,
-        lax.all_gather(features, "ex", axis=0, tiled=True),
+        jnp.concatenate(
+            lax.all_to_all(jnp.stack([features] * lax.axis_size("ex")), "ex", 0, 0), axis=0
+        ),
         preferred_element_type=jnp.float32,
     )
 

time: 1090 us -> 494 us (0.45)
  waiting for transfers between devices: 1060 us -> 75 us
  blocking collectives: 0 us -> 379 us
    all_gather x1 -> x0, waiting for transfers between devices: 982 us -> none  [body(): lax.all_gather(features, 'ex', axis=0, tiled=True)]
    all_to_all x0 -> x1, blocking collectives: none -> 379 us  [body(): lax.all_to_all(jnp.stack([features] * lax.axis_size('ex')), 'ex', 0, 0)]
  transfers between devices with their start and end apart: 2 -> 1, of which waited for: 2 -> 1; matrix products, arithmetic and copies ran while one was open for 0% -> 1% of each run, Pallas kernels for 0% -> 0%
where the time goes in v1:
time: 494 us; the launch traced here: 488 us
  blocking collectives  379 us (77%)
  waiting for transfers between devices  75 us (15%)
  between operations  13.5 us (3%)
  local copies, waits for them, and re-layouts  8.97 us (2%)
  matrix products  6.25 us (1%)
  other arithmetic  5.57 us (1%)
    all_to_all x1, blocking collectives, body(): lax.all_to_all(jnp.stack([features] * lax.axis_size('ex')), 'ex', 0, 0)  379 us
    all_gather x1, waiting for transfers between devices, body(): portion = lax.all_gather(proj_rows, 'tok', axis=0, tiled=True)  74.3 us
  transfers between devices with their start and end apart: 1, of which 1 were waited for; matrix products, arithmetic and copies ran while one was open for 1% of the time, Pallas kernels for 0%

profile of v1, /device:TPU:0, one launch (start us, length us, event | category | flops | bytes accessed | tf_op | source)
XLA Modules:
  0.0 488.5 jit_solution(7045535031229497827)
XLA Ops:
  6.5 0.0 copy-start
  6.5 0.0 all-gather.2.cloned.1.call-start
  6.5 0.7 all-gather.2.cloned.1.call-update
  7.3 0.7 copy.9
  8.0 0.1 reduce-window.8
  8.1 0.1 reduce
  8.2 0.9 select_reduce_fusion.1
  9.1 0.2 convert_reduce_fusion
  9.3 0.9 select_reduce_fusion
  10.2 74.3 %all-gather.2.cloned.1.call-done = bf16[8192,128]{1,0:T(8,128)(2,1)} async-done(((bf16[2048,128]{1,0:T(8,128)(2,1)}), bf16[8192,128]{1,0:T(8,128)(2,1)}) %all-gather.2.cloned.1.call-update) | async-done | bytes 2097168 | tf_op jit(solution)/shard_map/all_gather | solution.py:36
  84.5 4.3 fusion.7
  88.8 2.7 copy.10
  91.5 6.2 %while.10 = (s32[]{:T(128)}, f32[2,256,64]{1,2,0:T(8,128)S(1)}, s32[8192]{0:T(1024)S(1)}, s32[2,4]{1,0:T(2,128)S(1)}, bf16[8192,64]{0,1:T(8,128)(2,1)}, /*index=5*/bf16[8192,64]{1,0:T(8,128)(2,1)S(1)}, s32[]{:T(128)}) while((s32[]{:T(128)}, f32[2,256,64]{1,2,0:T(8,128)S(1)}, s32[8192]{0:T(1024)S(1)}, s32[2,4]{1,0:T(2,128)S(1)}, ...), condition=%wide.region_4.5_spmd, body=%wide.region_3.4_spmd.sunk | while | flops 270598144 | bytes 11763853 | solution.py:25
  91.5 0.1 compare_convert_fusion.2
  91.6 1.6 broadcast_multiply_fusion.2
  93.2 1.4 fusion.18
  94.6 0.1 compare_convert_fusion.2
  94.7 1.6 broadcast_multiply_fusion.2
  96.3 1.4 fusion.18
  97.7 0.1 copy.11
  97.9 0.1 reshape.87
  98.0 0.1 divide_convert_fusion
  98.1 1.0 stack.2
  99.1 379.2 %all_to_all.5 = bf16[128,8,4096]{2,1,0:T(8,128)(2,1)S(1)} all-to-all(bf16[128,8,4096]{2,1,0:T(8,128)(2,1)S(1)} %stack.2), channel_id=1, replica_groups=mesh['ex'=128,'tok'=4] {'ex'}, dimensions={0} | all-to-all | bytes 16777216 | tf_op jit(solution)/shard_map/all_to_all | solution.py:47
  478.3 0.0 copy-done
  478.3 3.4 fusion.4
  (6 shorter events, 0.0 us)
Async XLA Ops:
  6.5 471.7 %copy-start = (bf16[64,4096]{1,0:T(8,128)(2,1)S(1)}, bf16[64,4096]{1,0:T(8,128)(2,1)}, u32[]{:S(2)}) copy-start(bf16[64,4096]{1,0:T(8,128)(2,1)} %param.7) | copy-start | bytes 1572868
  6.5 78.0 %all-gather.2.cloned.1.call-start = ((), (), s32[]{:S(2)}) async-start(), calls=%async_computation.1 | async-start | bytes 2621440 | tf_op jit(solution)/shard_map/all_gather | solution.py:36
Sparse Core Ops, SparseCore 0:
  9.5 75.0 all-gather.1
